TPU v7x, 512 devices: a whole 4x8x8 slice. The times are simulated.
512 devices in a mesh: tensor: 8 (over x, core), dp: 64 (over y, z).
Axes of the slice: x: 4, y: 8, z: 8, core: 2. Of those that a mesh axis runs over, the one named last changes fastest.
Arguments:
- inputs: bfloat16 [16384, 8192], P('dp', 'tensor'), may hold values from -6 to 6
- frozen_value_weight: bfloat16 [8192, 1024], P(None, 'tensor'), may hold values from -0.0625 to 0.0625
- adapter_down_matrix: bfloat16 [64, 8192, 16], P('dp', 'tensor'), may hold values from -0.0625 to 0.0625
- adapter_up_matrix: bfloat16 [64, 16, 1024], P('dp', None, 'tensor'), may hold values from -1.5 to 1.5
- value_cotangent: bfloat16 [16384, 1024], P('dp', 'tensor'), may hold values from -6 to 6
- tenant_of_block: int32 [128], P('dp'), may hold values from 0 to 63
- quotas: int32 [64], replicated, may hold values from 128 to 1023
Outputs:
- adapted_values: bfloat16 [16384, 1024], P('dp', 'tensor')
- gradient_inputs: bfloat16 [16384, 8192], P('dp', 'tensor')
- down_grad: float32 [64, 8192, 16], P('dp', 'tensor')
- gradient_up_matrix: float32 [64, 16, 1024], P('dp', None, 'tensor')
All inputs are finite; a program needn't handle non-finite values.
Results may differ from a plain program's by a relative error of at most 0.015.
Values may be sent and summed in bfloat16 or wider, within the bound.
A program may use at most 64 MiB of HBM per device.

v0:
```python
import jax
import jax.numpy as jnp
from jax import lax
from jax.sharding import PartitionSpec as P

ADAPTER_RANK = 16
BLOCK = 128
adapter_scale = 2.0


def cut_along(value, dim, length):
    before, after = (value.shape[:dim], value.shape[dim + 1 :])
    return jnp.moveaxis(value.reshape(*before, length, -1, *after), dim, 0)


def sum_at_owner(value, axis, dim):
    length = lax.axis_size(axis)
    blocks = lax.all_to_all(cut_along(value, dim, length), axis, 0, 0, tiled=True)
    return jnp.sum(blocks.astype(jnp.float32), axis=0)


def laid_out(blocks, dim):
    blocks = jnp.moveaxis(blocks, 0, dim)
    shape = blocks.shape
    return blocks.reshape(*shape[:dim], shape[dim] * shape[dim + 1], *shape[dim + 2 :])


def sent_to_all(value, axis):
    copies = jnp.broadcast_to(value, (lax.axis_size(axis), *value.shape))
    return lax.all_to_all(copies, axis, split_axis=0, concat_axis=0, tiled=True)


def gather_directly(value, axis, dim):
    return laid_out(sent_to_all(value, axis), dim)


def sent_together(arrays, axis, dim, along):
    columns = [a.reshape(*a.shape[:along], -1) for a in arrays]
    both = jnp.concatenate(columns, axis=along)
    whole, at, outs = (lax.all_gather(both, axis, axis=dim, tiled=True), 0, [])
    for a, column in zip(arrays, columns):
        section = whole[..., at : at + column.shape[along]]
        outs.append(section.reshape(*section.shape[:along], *a.shape[along:]))
        at += column.shape[along]
    return tuple(outs)


def on_device(
    inputs,
    frozen_value_weight,
    adapter_down_matrix,
    adapter_up_matrix,
    value_cotangent,
    tenant_of_block,
    quotas,
):
    token_rows, local_features = inputs.shape
    local_values = frozen_value_weight.shape[1]
    nblocks = tenant_of_block.shape[0]
    owned_adapters = adapter_down_matrix.shape[0]
    adapter_count = owned_adapters * lax.axis_size("dp")
    groups = lax.axis_size("tensor")
    weight_rows = lax.all_to_all(
        frozen_value_weight, "tensor", split_axis=0, concat_axis=1, tiled=True
    )
    base_terms = jnp.dot(inputs, weight_rows, preferred_element_type=jnp.float32)
    frozen_output = sum_at_owner(base_terms.astype(jnp.bfloat16), "tensor", 1)
    grad_full = gather_directly(value_cotangent, "tensor", 1)
    summed_gradient = jnp.zeros((token_rows, local_features), jnp.float32)
    for index in range(groups):
        lower = index * local_values
        term = lax.dot_general(
            grad_full[:, lower : lower + local_values],
            weight_rows[:, lower : lower + local_values],
            (((1,), (1,)), ((), ())),
            preferred_element_type=jnp.float32,
        )
        summed_gradient = summed_gradient + term.astype(jnp.bfloat16).astype(jnp.float32)
    tenant_all = gather_directly(tenant_of_block, "dp", 0)
    down_all, up_all = (
        lax.all_gather(adapter_down_matrix, "dp", axis=0, tiled=True),
        lax.all_gather(adapter_up_matrix, "dp", axis=0, tiled=True),
    )
    down_blocks = down_all[tenant_of_block]
    up_blocks = up_all[tenant_of_block]
    input_blocks = inputs.reshape(nblocks, BLOCK, local_features)
    value_grad_blocks = value_cotangent.reshape(nblocks, BLOCK, local_values)
    low_part = jnp.einsum(
        "bnd,bdr->bnr", input_blocks, down_blocks, preferred_element_type=jnp.float32
    )
    gradient_portion = adapter_scale * jnp.einsum(
        "bnk,brk->bnr", value_grad_blocks, up_blocks, preferred_element_type=jnp.float32
    )
    low_sum, grad_sum = (
        lax.psum(low_part.astype(jnp.bfloat16), "tensor").astype(jnp.float32),
        lax.psum(gradient_portion.astype(jnp.bfloat16), "tensor").astype(jnp.float32),
    )
    reduced_features = low_sum.astype(jnp.bfloat16)
    gradient_lowrank = grad_sum.astype(jnp.bfloat16)
    raised_output = jnp.einsum(
        "bnr,brk->bnk", reduced_features, up_blocks, preferred_element_type=jnp.float32
    )
    adapted_values = (
        frozen_output + adapter_scale * raised_output.reshape(token_rows, local_values)
    ).astype(jnp.bfloat16)
    adapter_input = jnp.einsum(
        "bnr,bdr->bnd", gradient_lowrank, down_blocks, preferred_element_type=jnp.float32
    )
    gradient_inputs = (summed_gradient + adapter_input.reshape(token_rows, local_features)).astype(
        jnp.bfloat16
    )
    adapter_ids = jnp.arange(adapter_count, dtype=jnp.int32)
    counts = (
        jnp.sum((tenant_all[:, None] == adapter_ids[None, :]).astype(jnp.float32), axis=0) * BLOCK
    )
    scale = quotas.astype(jnp.float32) / jnp.maximum(counts, 1.0)
    local_hot = (tenant_of_block[:, None] == adapter_ids[None, :]).astype(jnp.float32)
    block_weight = jnp.dot(local_hot, scale, precision=lax.Precision.HIGHEST)
    grad_a = (
        jnp.einsum(
            "bnd,bnr->bdr", input_blocks, gradient_lowrank, preferred_element_type=jnp.float32
        )
        * block_weight[:, None, None]
    )
    up_gradient_local = (
        adapter_scale
        * jnp.einsum(
            "bnr,bnk->brk", reduced_features, value_grad_blocks, preferred_element_type=jnp.float32
        )
        * block_weight[:, None, None]
    )
    my_index = lax.axis_index("dp")
    first_owned = my_index * owned_adapters
    owned_ids = first_owned + jnp.arange(owned_adapters, dtype=jnp.int32)
    start_a = jnp.zeros((owned_adapters, local_features, ADAPTER_RANK), jnp.float32)
    start_b = jnp.zeros((owned_adapters, ADAPTER_RANK, local_values), jnp.float32)
    pieces = tuple(
        (
            part.astype(jnp.float32)
            for part in sent_together(
                (grad_a.astype(jnp.bfloat16), up_gradient_local.astype(jnp.bfloat16)), "dp", 0, 1
            )
        )
    )
    selector = (tenant_all[:, None] == owned_ids[None, :]).astype(jnp.float32)
    new_a = start_a + jnp.einsum(
        "bo,bdr->odr", selector, pieces[0], precision=lax.Precision.HIGHEST
    )
    new_b = start_b + jnp.einsum(
        "bo,brk->ork", selector, pieces[1], precision=lax.Precision.HIGHEST
    )
    return (adapted_values, gradient_inputs, new_a, new_b)


def solution(mesh):
    placed = (
        P("dp", "tensor"),
        P(None, "tensor"),
        P("dp", "tensor", None),
        P("dp", None, "tensor"),
        P("dp", "tensor"),
        P("dp"),
        P(),
    )
    return jax.shard_map(
        on_device,
        mesh=mesh,
        in_specs=placed,
        out_specs=(
            P("dp", "tensor"),
            P("dp", "tensor"),
            P("dp", "tensor", None),
            P("dp", None, "tensor"),
        ),
        check_vma=False,
    )
```

profile of v0, /device:TPU:2, one launch (start us, length us, event | category | flops | bytes accessed | tf_op | source)
XLA Modules:
  0.0 249.3 jit_solution(11249866176702770566)
XLA Ops:
  7.9 1.3 broadcast_in_dim.8
  9.2 16.6 %all-to-all-start.3 = ((s32[64,1,2]{2,1,0:T(1,128)}), s32[64,1,2]{2,1,0:T(1,128)S(1)}, u32[]{:S(2)}, u32[]{:S(2)}) async-start(s32[64,1,2]{2,1,0:T(1,128)} %broadcast_in_dim.8), calls=%async_computation.3 | async-start | bytes 65536 | tf_op jit(solution)/shard_map/all_to_all | solution.py:30
  25.9 50.4 %all_gather.10 = bf16[64,16,128]{2,1,0:T(8,128)(2,1)S(1)} all-gather(bf16[1,16,128]{2,1,0:T(8,128)(2,1)} %param.10), channel_id=1, replica_groups=mesh['tensor'=8,'dp'=64] {'dp'}, dimensions={0}, use_global_device_ids=true | all-gather | bytes 266240 | tf_op jit(solution)/shard_map/all_gather | solution.py:82
  77.4 1.0 fusion.23
  80.8 18.5 %all-gather.4.cloned.1.call-done = bf16[64,1024,16]{1,2,0:T(8,128)(2,1)} async-done(((bf16[1,1024,16]{1,2,0:T(8,128)(2,1)}), bf16[64,1024,16]{1,2,0:T(8,128)(2,1)}) %all-gather.4.cloned.1.call-update) | async-done | bytes 2097168 | tf_op jit(solution)/shard_map/all_gather | solution.py:81
  99.3 2.1 gather_fusion
  101.7 20.7 %all-reduce = (bf16[2,128,16]{1,2,0:T(8,128)(2,1)S(1)}, bf16[2,128,16]{1,2,0:T(8,128)(2,1)S(1)}) all-reduce(bf16[2,128,16]{1,2,0:T(8,128)(2,1)S(1)} %fusion.24, bf16[2,128,16]{1,2,0:T(8,128)(2,1)S(1)} %fusion.23), channel_id=1, replica_groups=mesh['tensor'=8,'dp'=64] {'tensor'}, use_global_device_ids=true, to_apply=%region_1.0 | all-reduce | flops 8192 | bytes 32768 | tf_op jit(solution)/shard_map/psum | solution.py:95
  124.2 7.0 %all-to-all-start = ((bf16[8,1024,128]{2,1,0:T(8,128)(2,1)}), bf16[8,1024,128]{2,1,0:T(8,128)(2,1)S(1)}, u32[]{:S(2)}, u32[]{:S(2)}) async-start(bf16[8,1024,128]{2,1,0:T(8,128)(2,1)} %bitcast.84), calls=%async_computation | async-start | bytes 4194304 | tf_op jit(solution)/shard_map/all_to_all | solution.py:63
  131.4 25.6 %all-to-all-done = bf16[8,1024,128]{2,1,0:T(8,128)(2,1)S(1)} async-done(((bf16[8,1024,128]{2,1,0:T(8,128)(2,1)}), bf16[8,1024,128]{2,1,0:T(8,128)(2,1)S(1)}, u32[]{:S(2)}, u32[]{:S(2)}) %all-to-all-start) | async-done | bytes 2097184 | tf_op jit(solution)/shard_map/all_to_all | solution.py:63
  157.9 4.8 %all-to-all-start.2 = ((bf16[8,256,128]{1,2,0:T(8,128)(2,1)}), bf16[8,256,128]{1,2,0:T(8,128)(2,1)S(1)}, u32[]{:S(2)}, u32[]{:S(2)}) async-start(bf16[8,256,128]{1,2,0:T(8,128)(2,1)} %broadcast_in_dim.7), calls=%async_computation.2 | async-start | bytes 1048576 | tf_op jit(solution)/shard_map/all_to_all | solution.py:30
  163.0 2.9 %copy.28 = bf16[1024,8,128]{0,2,1:T(8,128)(2,1)S(1)} copy(bf16[1024,8,128]{2,0,1:T(8,128)(2,1)} %bitcast.82) | data formatting | bytes 4194304 | tf_op jit(solution)/shard_map/all_to_all | solution.py:63
  167.5 4.1 %all-to-all-done.2 = bf16[8,256,128]{1,2,0:T(8,128)(2,1)S(1)} async-done(((bf16[8,256,128]{1,2,0:T(8,128)(2,1)}), bf16[8,256,128]{1,2,0:T(8,128)(2,1)S(1)}, u32[]{:S(2)}, u32[]{:S(2)}) %all-to-all-start.2) | async-done | bytes 524320 | tf_op jit(solution)/shard_map/all_to_all | solution.py:30
  172.4 4.9 %all-to-all-start.1 = ((bf16[8,256,128]{2,1,0:T(8,128)(2,1)}), bf16[8,256,128]{2,1,0:T(8,128)(2,1)S(1)}, u32[]{:S(2)}, u32[]{:S(2)}) async-start(bf16[8,256,128]{2,1,0:T(8,128)(2,1)} %bitcast.93), calls=%async_computation.1 | async-start | bytes 1048576 | tf_op jit(solution)/shard_map/all_to_all | solution.py:18
  177.3 1.2 fusion.16
  178.5 1.2 fusion.15
  180.9 1.3 fusion.5
  182.3 3.9 %all-to-all-done.1 = bf16[8,256,128]{2,1,0:T(8,128)(2,1)S(1)} async-done(((bf16[8,256,128]{2,1,0:T(8,128)(2,1)}), bf16[8,256,128]{2,1,0:T(8,128)(2,1)S(1)}, u32[]{:S(2)}, u32[]{:S(2)}) %all-to-all-start.1) | async-done | bytes 524320 | tf_op jit(solution)/shard_map/all_to_all | solution.py:18
  187.4 2.0 fusion.3
  189.4 19.9 %all-gather.6.cloned.1.call-done = bf16[64,2,18432]{2,1,0:T(2,128)(2,1)} async-done(((bf16[1,2,18432]{2,1,0:T(2,128)(2,1)}), bf16[64,2,18432]{2,1,0:T(2,128)(2,1)}) %all-gather.6.cloned.1.call-update) | async-done | bytes 4718608 | tf_op jit(solution)/shard_map/all_gather | solution.py:40
  209.3 7.6 %reshape.94 = bf16[128,18432]{1,0:T(8,128)(2,1)} reshape(bf16[64,2,18432]{2,1,0:T(2,128)(2,1)} %all-gather.6.cloned.1.call-done) | data formatting | bytes 9437184
  216.8 4.5 %slice.92 = bf16[128,16384]{1,0:T(8,128)(2,1)} slice(bf16[128,18432]{1,0:T(8,128)(2,1)} %reshape.94), slice={[0:128], [0:16384]} | slice | bytes 8388608 | tf_op jit(solution)/shard_map/slice | solution.py:42
  221.3 1.8 fusion.25
  223.2 6.4 %copy.32 = bf16[128,16384]{0,1:T(8,128)(2,1)} copy(bf16[128,16384]{1,0:T(8,128)(2,1)} %slice.92) | data formatting | bytes 8388608 | tf_op jit(solution)/shard_map/slice | solution.py:42
  229.6 12.0 %fusion.55 = f32[1,1024,16]{2,0,1:T(1,128)S(1)} fusion(pred[128,1,1]{0,1,2:T(4,128)(4,1)S(1)} %reshape.97, bf16[128,1024,16]{0,2,1:T(8,128)(2,1)} %bitcast.72), kind=kOutput, calls=%fused_computation.84 | convolution fusion | flops 4194304 | bytes 4259968 | tf_op jit(solution)/shard_map/bo,bdr->odr/dot_general | solution.py:146
  (47 shorter events, 13.6 us)
Async XLA Ops:
  7.2 94.3 %copy-start = (bf16[256,1024]{1,0:T(8,128)(2,1)S(1)}, bf16[256,1024]{1,0:T(8,128)(2,1)}, u32[]{:S(2)}) copy-start(bf16[256,1024]{1,0:T(8,128)(2,1)} %param.7) | copy-start | bytes 1572868
  7.2 115.2 %copy-start.5 = (bf16[256,128]{1,0:T(8,128)(2,1)S(1)}, bf16[256,128]{1,0:T(8,128)(2,1)}, u32[]{:S(2)}) copy-start(bf16[256,128]{1,0:T(8,128)(2,1)} %param.11) | copy-start | bytes 196612
  7.2 92.1 %all-gather.4.cloned.1.call-start = ((), (), s32[]{:S(2)}) async-start(), calls=%async_computation.4 | async-start | bytes 2129920 | tf_op jit(solution)/shard_map/all_gather | solution.py:81
  9.2 69.2 %all-to-all-start.3 = ((s32[64,1,2]{2,1,0:T(1,128)}), s32[64,1,2]{2,1,0:T(1,128)S(1)}, u32[]{:S(2)}, u32[]{:S(2)}) async-start(s32[64,1,2]{2,1,0:T(1,128)} %broadcast_in_dim.8), calls=%async_computation.3 | async-start | bytes 65536 | tf_op jit(solution)/shard_map/all_to_all | solution.py:30
  25.8 183.5 %all-gather.6.cloned.1.call-start = ((), (), s32[]{:S(2)}) async-start(), calls=%async_computation.5 | async-start | bytes 4792320 | tf_op jit(solution)/shard_map/all_gather | solution.py:40
  124.2 32.7 %all-to-all-start = ((bf16[8,1024,128]{2,1,0:T(8,128)(2,1)}), bf16[8,1024,128]{2,1,0:T(8,128)(2,1)S(1)}, u32[]{:S(2)}, u32[]{:S(2)}) async-start(bf16[8,1024,128]{2,1,0:T(8,128)(2,1)} %bitcast.84), calls=%async_computation | async-start | bytes 4194304 | tf_op jit(solution)/shard_map/all_to_all | solution.py:63
  157.0 6.0 %copy-start.1 = (bf16[8,1024,128]{2,1,0:T(8,128)(2,1)}, bf16[8,1024,128]{2,1,0:T(8,128)(2,1)S(1)}, u32[]{:S(2)}) copy-start(bf16[8,1024,128]{2,1,0:T(8,128)(2,1)S(1)} %all-to-all-done) | copy-start | bytes 6291460
  157.9 13.7 %all-to-all-start.2 = ((bf16[8,256,128]{1,2,0:T(8,128)(2,1)}), bf16[8,256,128]{1,2,0:T(8,128)(2,1)S(1)}, u32[]{:S(2)}, u32[]{:S(2)}) async-start(bf16[8,256,128]{1,2,0:T(8,128)(2,1)} %broadcast_in_dim.7), calls=%async_computation.2 | async-start | bytes 1048576 | tf_op jit(solution)/shard_map/all_to_all | solution.py:30
  171.6 0.8 copy-start.3
  172.4 13.7 %all-to-all-start.1 = ((bf16[8,256,128]{2,1,0:T(8,128)(2,1)}), bf16[8,256,128]{2,1,0:T(8,128)(2,1)S(1)}, u32[]{:S(2)}, u32[]{:S(2)}) async-start(bf16[8,256,128]{2,1,0:T(8,128)(2,1)} %bitcast.93), calls=%async_computation.1 | async-start | bytes 1048576 | tf_op jit(solution)/shard_map/all_to_all | solution.py:18
  177.3 2.4 copy-start.4
  186.2 1.3 copy-start.2
Sparse Core Ops, SparseCore 0:
  11.0 88.2 all-gather.3
  124.4 84.8 all-gather.5
where the time goes:
time: 250 us; the launch traced here: 249 us
  waiting for transfers between devices  72.7 us (29%)
  blocking collectives  71 us (28%)
  starting transfers between devices  33.4 us (13%)
  local copies, waits for them, and re-layouts  30.6 us (12%)
  matrix products  24.4 us (10%)
  between operations  14.2 us (6%)
  other arithmetic  3.02 us (1%)
    all_gather x1, blocking collectives, on_device(): lax.all_gather(adapter_up_matrix, 'dp', axis=0, tiled=True)  50.4 us
    all_to_all x1, waiting for transfers between devices, on_device(): lax.all_to_all(frozen_value_weight, 'tensor', split_axis=0, concat_axis=1...  25.6 us
    all_to_all x2, starting transfers between devices, sent_to_all(): return lax.all_to_all(copies, axis, split_axis=0, concat_axis=0, tiled=True)  21.4 us
    psum x1, blocking collectives, on_device(): lax.psum(low_part.astype(jnp.bfloat16), 'tensor').astype(jnp.float32)  20.7 us
    all_gather x1, waiting for transfers between devices, sent_together(): whole, at, outs = (lax.all_gather(both, axis, axis=dim, tiled=True), 0, [])  19.9 us
    all_gather x1, waiting for transfers between devices, on_device(): lax.all_gather(adapter_down_matrix, 'dp', axis=0, tiled=True)  18.5 us
    dot_general x1, matrix products, on_device(): jnp.einsum('bo,bdr->odr', selector, pieces[0], precision=lax.Precision.HI...  12 us
    slice x2, local copies, waits for them, and re-layouts, sent_together(): section = whole[..., at:at + column.shape[along]]  10.9 us
  transfers between devices with their start and end apart: 6, of which 5 were waited for; matrix products, arithmetic and copies ran while one was open for 8% of the time, Pallas kernels for 0%

commit v1 on v0

--- a/solution.py
+++ b/solution.py
@@ -92,7 +92,9 @@
         "bnk,brk->bnr", value_grad_blocks, up_blocks, preferred_element_type=jnp.float32
     )
     low_sum, grad_sum = (
-        lax.psum(low_part.astype(jnp.bfloat16), "tensor").astype(jnp.float32),
+        jnp.sum(lax.all_gather(low_part.astype(jnp.bfloat16), "tensor"), axis=0).astype(
+            jnp.float32
+        ),
         lax.psum(gradient_portion.astype(jnp.bfloat16), "tensor").astype(jnp.float32),
     )
     reduced_features = low_sum.astype(jnp.bfloat16)

time: 250 us -> 241 us (0.964)
  waiting for transfers between devices: 72.7 us -> 61.8 us
  blocking collectives: 71 us -> 74.3 us
    all_gather x0 -> x1, blocking collectives: none -> 12.8 us  [on_device(): lax.all_gather(low_part.astype(jnp.bfloat16), 'tensor')]
    all_gather x1, waiting for transfers between devices: 18.5 us -> 6.25 us  [on_device(): lax.all_gather(adapter_down_matrix, 'dp', axis=0, tiled=True)]
    psum x1, blocking collectives: 20.7 us -> 11.1 us  [on_device(): lax.psum(gradient_portion.astype(jnp.bfloat16), 'tensor')]
  transfers between devices with their start and end apart: 6 -> 6, of which waited for: 5 -> 5; matrix products, arithmetic and copies ran while one was open for 8% -> 9% of each run, Pallas kernels for 0% -> 0%
where the time goes in v1:
time: 241 us; the launch traced here: 239 us
  blocking collectives  74.3 us (31%)
  waiting for transfers between devices  61.8 us (26%)
  starting transfers between devices  31 us (13%)
  local copies, waits for them, and re-layouts  30.6 us (13%)
  matrix products  24.4 us (10%)
  between operations  14.2 us (6%)
  other arithmetic  3.05 us (1%)
    all_gather x1, blocking collectives, on_device(): lax.all_gather(adapter_up_matrix, 'dp', axis=0, tiled=True)  50.5 us
    all_to_all x1, waiting for transfers between devices, on_device(): lax.all_to_all(frozen_value_weight, 'tensor', split_axis=0, concat_axis=1...  25.6 us
    all_to_all x2, starting transfers between devices, sent_to_all(): return lax.all_to_all(copies, axis, split_axis=0, concat_axis=0, tiled=True)  21.6 us
    all_gather x1, waiting for transfers between devices, sent_together(): whole, at, outs = (lax.all_gather(both, axis, axis=dim, tiled=True), 0, [])  21.3 us
    all_gather x1, blocking collectives, on_device(): lax.all_gather(low_part.astype(jnp.bfloat16), 'tensor')  12.8 us
    dot_general x1, matrix products, on_device(): jnp.einsum('bo,bdr->odr', selector, pieces[0], precision=lax.Precision.HI...  12 us
    psum x1, blocking collectives, on_device(): lax.psum(gradient_portion.astype(jnp.bfloat16), 'tensor')  11.1 us
    slice x2, local copies, waits for them, and re-layouts, sent_together(): section = whole[..., at:at + column.shape[along]]  10.9 us
  transfers between devices with their start and end apart: 6, of which 5 were waited for; matrix products, arithmetic and copies ran while one was open for 9% of the time, Pallas kernels for 0%

profile of v1, /device:TPU:2, one launch (start us, length us, event | category | flops | bytes accessed | tf_op | source)
XLA Modules:
  0.0 239.4 jit_solution(12827711475067681387)
XLA Ops:
  7.9 1.3 broadcast_in_dim.8
  9.2 16.7 %all-to-all-start.3 = ((s32[64,1,2]{2,1,0:T(1,128)}), s32[64,1,2]{2,1,0:T(1,128)S(1)}, u32[]{:S(2)}, u32[]{:S(2)}) async-start(s32[64,1,2]{2,1,0:T(1,128)} %broadcast_in_dim.8), calls=%async_computation.3 | async-start | bytes 65536 | tf_op jit(solution)/shard_map/all_to_all | solution.py:30
  26.0 50.5 %all_gather.18 = bf16[64,16,128]{2,1,0:T(8,128)(2,1)S(1)} all-gather(bf16[1,16,128]{2,1,0:T(8,128)(2,1)} %param.10), channel_id=1, replica_groups=mesh['tensor'=8,'dp'=64] {'dp'}, dimensions={0}, use_global_device_ids=true | all-gather | bytes 266240 | tf_op jit(solution)/shard_map/all_gather | solution.py:82
  78.6 11.1 %psum.7 = bf16[2,128,16]{1,2,0:T(8,128)(2,1)S(1)} all-reduce(bf16[2,128,16]{1,2,0:T(8,128)(2,1)S(1)} %fusion.23), channel_id=1, replica_groups=mesh['tensor'=8,'dp'=64] {'tensor'}, use_global_device_ids=true, to_apply=%region_2.0 | all-reduce | flops 4096 | bytes 16384 | tf_op jit(solution)/shard_map/psum | solution.py:98
  93.1 6.2 %all-gather.5.cloned.1.call-done = bf16[64,1024,16]{1,2,0:T(8,128)(2,1)} async-done(((bf16[1,1024,16]{1,2,0:T(8,128)(2,1)}), bf16[64,1024,16]{1,2,0:T(8,128)(2,1)}) %all-gather.5.cloned.1.call-update) | async-done | bytes 2097168 | tf_op jit(solution)/shard_map/all_gather | solution.py:81
  99.4 2.1 gather_fusion
  101.8 12.8 %all-gather = bf16[16,128,16]{1,2,0:T(8,128)(2,1)S(1)} all-gather(bf16[2,128,16]{1,2,0:T(8,128)(2,1)S(1)} %fusion.24), channel_id=2, replica_groups=mesh['tensor'=8,'dp'=64] {'tensor'}, dimensions={0}, use_global_device_ids=true | all-gather | bytes 73728 | tf_op jit(solution)/shard_map/all_gather | solution.py:95
  115.4 4.5 %all-to-all-start = ((bf16[8,1024,128]{2,1,0:T(8,128)(2,1)}), bf16[8,1024,128]{2,1,0:T(8,128)(2,1)S(1)}, u32[]{:S(2)}, u32[]{:S(2)}) async-start(bf16[8,1024,128]{2,1,0:T(8,128)(2,1)} %bitcast.85), calls=%async_computation | async-start | bytes 4194304 | tf_op jit(solution)/shard_map/all_to_all | solution.py:63
  120.0 25.6 %all-to-all-done = bf16[8,1024,128]{2,1,0:T(8,128)(2,1)S(1)} async-done(((bf16[8,1024,128]{2,1,0:T(8,128)(2,1)}), bf16[8,1024,128]{2,1,0:T(8,128)(2,1)S(1)}, u32[]{:S(2)}, u32[]{:S(2)}) %all-to-all-start) | async-done | bytes 2097184 | tf_op jit(solution)/shard_map/all_to_all | solution.py:63
  146.5 4.9 %all-to-all-start.2 = ((bf16[8,256,128]{1,2,0:T(8,128)(2,1)}), bf16[8,256,128]{1,2,0:T(8,128)(2,1)S(1)}, u32[]{:S(2)}, u32[]{:S(2)}) async-start(bf16[8,256,128]{1,2,0:T(8,128)(2,1)} %broadcast_in_dim.7), calls=%async_computation.2 | async-start | bytes 1048576 | tf_op jit(solution)/shard_map/all_to_all | solution.py:30
  151.7 2.9 %copy.28 = bf16[1024,8,128]{0,2,1:T(8,128)(2,1)S(1)} copy(bf16[1024,8,128]{2,0,1:T(8,128)(2,1)} %bitcast.83) | data formatting | bytes 4194304 | tf_op jit(solution)/shard_map/all_to_all | solution.py:63
  156.2 4.1 %all-to-all-done.2 = bf16[8,256,128]{1,2,0:T(8,128)(2,1)S(1)} async-done(((bf16[8,256,128]{1,2,0:T(8,128)(2,1)}), bf16[8,256,128]{1,2,0:T(8,128)(2,1)S(1)}, u32[]{:S(2)}, u32[]{:S(2)}) %all-to-all-start.2) | async-done | bytes 524320 | tf_op jit(solution)/shard_map/all_to_all | solution.py:30
  161.1 4.9 %all-to-all-start.1 = ((bf16[8,256,128]{2,1,0:T(8,128)(2,1)}), bf16[8,256,128]{2,1,0:T(8,128)(2,1)S(1)}, u32[]{:S(2)}, u32[]{:S(2)}) async-start(bf16[8,256,128]{2,1,0:T(8,128)(2,1)} %bitcast.94), calls=%async_computation.1 | async-start | bytes 1048576 | tf_op jit(solution)/shard_map/all_to_all | solution.py:18
  165.9 1.2 fusion.16
  167.2 1.2 fusion.15
  169.6 1.4 fusion.5
  171.0 3.9 %all-to-all-done.1 = bf16[8,256,128]{2,1,0:T(8,128)(2,1)S(1)} async-done(((bf16[8,256,128]{2,1,0:T(8,128)(2,1)}), bf16[8,256,128]{2,1,0:T(8,128)(2,1)S(1)}, u32[]{:S(2)}, u32[]{:S(2)}) %all-to-all-start.1) | async-done | bytes 524320 | tf_op jit(solution)/shard_map/all_to_all | solution.py:18
  176.1 2.0 fusion.3
  178.1 21.3 %all-gather.7.cloned.1.call-done = bf16[64,2,18432]{2,1,0:T(2,128)(2,1)} async-done(((bf16[1,2,18432]{2,1,0:T(2,128)(2,1)}), bf16[64,2,18432]{2,1,0:T(2,128)(2,1)}) %all-gather.7.cloned.1.call-update) | async-done | bytes 4718608 | tf_op jit(solution)/shard_map/all_gather | solution.py:40
  199.4 7.6 %reshape.95 = bf16[128,18432]{1,0:T(8,128)(2,1)} reshape(bf16[64,2,18432]{2,1,0:T(2,128)(2,1)} %all-gather.7.cloned.1.call-done) | data formatting | bytes 9437184
  206.9 4.5 %slice.92 = bf16[128,16384]{1,0:T(8,128)(2,1)} slice(bf16[128,18432]{1,0:T(8,128)(2,1)} %reshape.95), slice={[0:128], [0:16384]} | slice | bytes 8388608 | tf_op jit(solution)/shard_map/slice | solution.py:42
  211.4 1.8 fusion.25
  213.3 6.4 %copy.32 = bf16[128,16384]{0,1:T(8,128)(2,1)} copy(bf16[128,16384]{1,0:T(8,128)(2,1)} %slice.92) | data formatting | bytes 8388608 | tf_op jit(solution)/shard_map/slice | solution.py:42
  219.7 12.0 %fusion.55 = f32[1,1024,16]{2,0,1:T(1,128)S(1)} fusion(pred[128,1,1]{0,1,2:T(4,128)(4,1)S(1)} %reshape.98, bf16[128,1024,16]{0,2,1:T(8,128)(2,1)} %bitcast.73), kind=kOutput, calls=%fused_computation.84 | convolution fusion | flops 4194304 | bytes 4259968 | tf_op jit(solution)/shard_map/bo,bdr->odr/dot_general | solution.py:148
  (49 shorter events, 14.6 us)
Async XLA Ops:
  7.2 84.9 %copy-start = (bf16[256,1024]{1,0:T(8,128)(2,1)S(1)}, bf16[256,1024]{1,0:T(8,128)(2,1)}, u32[]{:S(2)}) copy-start(bf16[256,1024]{1,0:T(8,128)(2,1)} %param.7) | copy-start | bytes 1572868
  7.2 92.2 %all-gather.5.cloned.1.call-start = ((), (), s32[]{:S(2)}) async-start(), calls=%async_computation.4 | async-start | bytes 2129920 | tf_op jit(solution)/shard_map/all_gather | solution.py:81
  9.2 105.3 %copy-start.5 = (bf16[256,128]{1,0:T(8,128)(2,1)S(1)}, bf16[256,128]{1,0:T(8,128)(2,1)}, u32[]{:S(2)}) copy-start(bf16[256,128]{1,0:T(8,128)(2,1)} %param.11) | copy-start | bytes 196612
  9.2 80.5 %all-to-all-start.3 = ((s32[64,1,2]{2,1,0:T(1,128)}), s32[64,1,2]{2,1,0:T(1,128)S(1)}, u32[]{:S(2)}, u32[]{:S(2)}) async-start(s32[64,1,2]{2,1,0:T(1,128)} %broadcast_in_dim.8), calls=%async_computation.3 | async-start | bytes 65536 | tf_op jit(solution)/shard_map/all_to_all | solution.py:30
  25.9 173.4 %all-gather.7.cloned.1.call-start = ((), (), s32[]{:S(2)}) async-start(), calls=%async_computation.5 | async-start | bytes 4792320 | tf_op jit(solution)/shard_map/all_gather | solution.py:40
  115.4 30.2 %all-to-all-start = ((bf16[8,1024,128]{2,1,0:T(8,128)(2,1)}), bf16[8,1024,128]{2,1,0:T(8,128)(2,1)S(1)}, u32[]{:S(2)}, u32[]{:S(2)}) async-start(bf16[8,1024,128]{2,1,0:T(8,128)(2,1)} %bitcast.85), calls=%async_computation | async-start | bytes 4194304 | tf_op jit(solution)/shard_map/all_to_all | solution.py:63
  145.6 6.0 %copy-start.1 = (bf16[8,1024,128]{2,1,0:T(8,128)(2,1)}, bf16[8,1024,128]{2,1,0:T(8,128)(2,1)S(1)}, u32[]{:S(2)}) copy-start(bf16[8,1024,128]{2,1,0:T(8,128)(2,1)S(1)} %all-to-all-done) | copy-start | bytes 6291460
  146.5 13.8 %all-to-all-start.2 = ((bf16[8,256,128]{1,2,0:T(8,128)(2,1)}), bf16[8,256,128]{1,2,0:T(8,128)(2,1)S(1)}, u32[]{:S(2)}, u32[]{:S(2)}) async-start(bf16[8,256,128]{1,2,0:T(8,128)(2,1)} %broadcast_in_dim.7), calls=%async_computation.2 | async-start | bytes 1048576 | tf_op jit(solution)/shard_map/all_to_all | solution.py:30
  160.3 0.8 copy-start.3
  161.1 13.7 %all-to-all-start.1 = ((bf16[8,256,128]{2,1,0:T(8,128)(2,1)}), bf16[8,256,128]{2,1,0:T(8,128)(2,1)S(1)}, u32[]{:S(2)}, u32[]{:S(2)}) async-start(bf16[8,256,128]{2,1,0:T(8,128)(2,1)} %bitcast.94), calls=%async_computation.1 | async-start | bytes 1048576 | tf_op jit(solution)/shard_map/all_to_all | solution.py:18
  165.9 2.4 copy-start.4
  174.8 1.3 copy-start.2
Sparse Core Ops, SparseCore 0:
  11.0 88.3 all-gather.4
  115.5 83.7 all-gather.6
